TPU v7x, 32 devices: a whole 2x2x4 slice. The times are simulated.
32 devices in a mesh: dp: 16 (over z, x, core), tensor: 2 (over y).
Axes of the slice: x: 2, y: 2, z: 4, core: 2. Of those that a mesh axis runs over, the one named last changes fastest.
Arguments:
- hidden_in: bfloat16 [16, 561, 1024], P('dp', None, 'tensor'), may hold values from -6 to 6
- lengths: int32 [16], P('dp'), may hold values from 52 to 512, as said below
- boxes: int32 [16, 561, 2], P('dp'), may hold values from 0 to 1000
- w_qkv: bfloat16 [1024, 3, 1024], P(None, None, 'tensor'), may hold values from -0.1875 to 0.1875
- w_out: bfloat16 [1024, 1024], P('tensor'), may hold values from -1 to 1
- w_up: bfloat16 [1024, 4096], P(None, 'tensor'), may hold values from -0.1875 to 0.1875
- w_down: bfloat16 [4096, 1024], P('tensor'), may hold values from -0.09375 to 0.09375
- rel_keys: bfloat16 [3, 128, 1024], P(None, None, 'tensor'), may hold values from -6 to 6
- rel_queries: bfloat16 [3, 128, 1024], P(None, None, 'tensor'), may hold values from -6 to 6
- norm_gains: float32 [2, 1024], P(None, 'tensor'), may hold values from 0.25 to 1.75
- norm_shifts: float32 [2, 1024], P(None, 'tensor'), may hold values from -3 to 3
- out_grad: bfloat16 [16, 561, 1024], P('dp', None, 'tensor'), may hold values from -6 to 6
Outputs:
- hidden_out: bfloat16 [16, 561, 1024], P('dp', None, 'tensor')
- input_grad: bfloat16 [16, 561, 1024], P('dp', None, 'tensor')
- qkv_grad: float32 [1024, 3, 1024], P(None, None, 'tensor')
- out_weight_grad: float32 [1024, 1024], P('tensor')
- up_grad: float32 [1024, 4096], P(None, 'tensor')
- down_grad: float32 [4096, 1024], P('tensor')
- rel_keys_grad: float32 [3, 128, 1024], P(None, None, 'tensor')
- rel_queries_grad: float32 [3, 128, 1024], P(None, None, 'tensor')
- gains_grad: float32 [2, 1024], P(None, 'tensor')
- shifts_grad: float32 [2, 1024], P(None, 'tensor')
Inputs may be any that keep to these rules, and one draw needn't show every extreme that they name: `lengths`: text slot s of a document holds a real token when s is under its count; in every draw some document has all 512 text slots real.
All inputs are finite; a program needn't handle non-finite values.
Results may differ from a plain program's by a relative error of at most 0.02.
Values may be sent and summed in bfloat16 or wider, within the bound.
No kernel may reach another device: no remote copies, remote signals or barrier semaphores. Data moves between devices by JAX's collectives and lax.ppermute only.
A program may use at most 512 MiB of HBM per device.

v0:
```python
import math, functools
import jax, jax.numpy as jnp
from jax import lax
from jax.sharding import PartitionSpec as P
from jax.experimental import pallas as pl
from jax.experimental.pallas import tpu as pltpu

HEAD_DIM = 64
BUCKETS = 128
TEXT = 512
NEG = -1e30
LOG2E = math.log2(math.e)
SCALE = 1.0 / math.sqrt(3 * HEAD_DIM)
F32 = jnp.float32
BF16 = jnp.bfloat16


def nt(a, b):
    return lax.dot_general(a, b, (((1,), (1,)), ((), ())), preferred_element_type=F32)


def nn(a, b):
    return lax.dot_general(a, b, (((1,), (0,)), ((), ())), preferred_element_type=F32)


def iota(shape, d):
    return lax.broadcasted_iota(jnp.int32, shape, d)


def each(n, body, straight):
    if straight:
        for b in range(n):
            body(b, 0)
    else:
        lax.fori_loop(0, n, body, 0)


def at_block(b, size):
    return b * size if isinstance(b, int) else pl.multiple_of(b * size, size)


def pick(table, index):
    return jnp.take_along_axis(table, index, axis=1, mode="promise_in_bounds")


def pick(table, index):
    dims = lax.GatherDimensionNumbers(
        offset_dims=(), collapsed_slice_dims=(1,), start_index_map=(1,),
        operand_batching_dims=(0,), start_indices_batching_dims=(0,))
    return lax.gather(table, index[..., None], dims, slice_sizes=(1, 1),
                      mode=lax.GatherScatterMode.PROMISE_IN_BOUNDS)


LEVELS = 10900.0
HALF_WORD = 65536.0


def tall_block(rows):
    return next(n for n in (288, 192, 128, 64) if rows % n == 0)


def fwd_kernel(slots, sp, rp, len_ref, q_ref, k_ref, v_ref, relk_ref, relq_ref, bc_ref, br_ref,
               ctx_ref, p_ref, qs, ks, vs, kt, idx, nq, nk, sq, fq, fk, gk, cs):
    pair = pl.program_id(1)
    nb = sp // 128
    tall = tall_block(rp)

    @pl.when(pair == 0)
    def _():
        qs[...] = jnp.zeros_like(qs)
        ks[...] = jnp.zeros_like(ks)
        vs[...] = jnp.zeros_like(vs)

        def rows(b, c):
            r0 = at_block(b, 128)
            row = iota((128, sp), 0) + r0
            col = iota((128, sp), 1)
            idx[0, pl.ds(r0, 128), :] = jnp.clip(col - row, -64, 63) + 64
            for t in range(2):
                x_i = bc_ref[pl.ds(r0, 128), t:t + 1]
                x_j = br_ref[t:t + 1, :]
                idx[t + 1, pl.ds(r0, 128), :] = jnp.clip((x_j - x_i) >> 4, -64, 63) + 64
            return c
        lax.fori_loop(0, nb, rows, 0)

    qs[0:slots, :] = q_ref[...]
    ks[0:slots, :] = k_ref[...]
    vs[0:slots, :] = v_ref[...]
    kt[...] = ks[...].T
    place = iota((1, sp), 1)
    length = len_ref[pl.program_id(0)]
    barred = jnp.where((place < length) | ((place >= TEXT) & (place < slots)), 0.0, NEG)
    half = iota((1, 128), 1) < 64

    def longest(rel_ref, h):
        rel = rel_ref[h * 64:(h + 1) * 64, :].astype(F32)
        return jnp.max(jnp.sum(rel * rel, axis=0, keepdims=True), axis=1, keepdims=True) * 1.03

    def bound(squares, most):
        return jnp.maximum(squares * most, 1e-30)

    member = jnp.where((iota((128, 256), 0) < 64) == (iota((128, 256), 1) < 128), 1.0, 0.0).astype(BF16)
    for side, (rows_ref, rel_ref, table) in enumerate(((qs, relk_ref, nq), (ks, relq_ref, nk))):
        most = [longest(rel_ref, h) for h in range(2)]
        if side == 1:
            most_k = most

        def pack(b, c):
            r0 = at_block(b, tall)
            here = rows_ref[pl.ds(r0, tall), :]
            wide = here.astype(F32)
            squares = nn((wide * wide).astype(BF16), member)
            words = []
            for h in range(2):
                mine = half if h == 0 else jnp.logical_not(half)
                top = bound(squares[:, h * 128:(h + 1) * 128], most[h])
                inverse = lax.rsqrt(top)
                if side == 0:
                    sq[h, pl.ds(r0, tall), :] = top * inverse * (1.0 / (LEVELS * HALF_WORD))
                inverse = inverse * LEVELS
                near = nn(jnp.where(mine, here, 0), rel_ref[...])
                words.append(jnp.round(near * jnp.concatenate([inverse] * 3, axis=1)).astype(jnp.int32))
            table[pl.ds(r0, tall), :] = (words[0] << 16) + words[1]
            return c
        each(rp // tall, pack, True)

    turned = kt[...].astype(F32)
    turned = (turned * turned).astype(BF16)
    pick_head = jnp.where((iota((16, 128), 0) < 8) == (iota((16, 128), 1) < 64), 1.0, 0.0).astype(BF16)
    squares = nn(pick_head, turned)
    step_k = [jnp.sqrt(bound(squares[h * 8:h * 8 + 1, :], most_k[h])) * (1.0 / (LEVELS * HALF_WORD)) for h in range(2)]

    def near(r0, count):
        for r in range(0, count, 8):
            here = pl.ds(r0 + r if isinstance(r0, int) else pl.multiple_of(r0 + r, 8), 8)
            for jb in range(nb):
                at = slice(jb * 128, (jb + 1) * 128)
                sums = [None] * 2
                for t in range(3):
                    ix = idx[t, here, at]
                    kind = slice(t * 128, (t + 1) * 128)
                    for n, table in enumerate((nq, nk)):
                        e = pick(table[here, kind], ix)
                        sums[n] = e if sums[n] is None else sums[n] + e
                fq[here, at] = sums[0]
                gk[r:r + 8, at] = sums[1]
        for jb in range(nb):
            at = slice(jb * 128, (jb + 1) * 128)
            fk[at, pl.ds(r0, 128)] = gk[:, at].T

    def near_block(b, c):
        near(at_block(b, 128), 128)
        return c
    each(rp // 128, near_block, True)
    if rp % 128:
        gk[rp % 128:, :] = jnp.zeros((128 - rp % 128, sp), jnp.int32)
        near(rp // 128 * 128, rp % 128)

    def soft(b, c):
        r0 = at_block(b, tall)
        for h in range(2):
            mine = half if h == 0 else jnp.logical_not(half)
            q_b = jnp.where(mine, qs[pl.ds(r0, tall), :], 0)
            from_q = fq[pl.ds(r0, tall), :]
            from_k = fk[pl.ds(r0, tall), :]
            if h == 1:
                from_q = from_q << 16
                from_k = from_k << 16
            step_q = jnp.concatenate([sq[h, pl.ds(r0, tall), :]] * nb, axis=1)
            s = (nn(q_b, kt[...]) + barred) + (from_q.astype(F32) * step_q + from_k.astype(F32) * step_k[h])
            m = jnp.max(s, axis=1, keepdims=True)
            e = jnp.exp2((s - m) * (SCALE * LOG2E))
            tot = jnp.sum(e, axis=1, keepdims=True)
            p = (e * (1.0 / tot)).astype(BF16)
            p_ref[h, pl.ds(r0, tall), :] = p
            got = nn(p, vs[...])
            if h == 0:
                first = got
            else:
                cs[pl.ds(r0, tall), :] = jnp.where(mine, got, first).astype(BF16)
        return c
    each(rp // tall, soft, False)
    ctx_ref[...] = cs[0:slots, :]


def attend_forward(lengths, qkv, relk, relq, boxes_col, boxes_row, heads):
    docs, slots, width = qkv.shape
    width = width // 3
    sp = boxes_row.shape[2]
    rp = -(-slots // 64) * 64
    pairs = heads // 2

    def part(t):
        return pl.BlockSpec((None, slots, 128), lambda d, p, ln: (d, 0, t * pairs + p))
    rel = pl.BlockSpec((128, 3 * BUCKETS), lambda d, p, ln: (p, 0))
    grid_spec = pltpu.PrefetchScalarGridSpec(
        num_scalar_prefetch=1, grid=(docs, pairs),
        in_specs=[part(0), part(1), part(2), rel, rel,
                  pl.BlockSpec((None, sp, 2), lambda d, p, ln: (d, 0, 0)),
                  pl.BlockSpec((None, 2, sp), lambda d, p, ln: (d, 0, 0))],
        out_specs=[pl.BlockSpec((None, slots, 128), lambda d, p, ln: (d, 0, p)),
                   pl.BlockSpec((None, 2, rp, sp), lambda d, p, ln: (d, p, 0, 0))],
        scratch_shapes=[pltpu.VMEM((sp, 128), BF16)] * 3 + [pltpu.VMEM((128, sp), BF16)]
        + [pltpu.VMEM((3, sp, sp), jnp.int32), pltpu.VMEM((sp, 384), jnp.int32), pltpu.VMEM((sp, 384), jnp.int32),
           pltpu.VMEM((2, sp, 128), F32), pltpu.VMEM((sp, sp), jnp.int32), pltpu.VMEM((sp, sp), jnp.int32),
           pltpu.VMEM((128, sp), jnp.int32), pltpu.VMEM((rp, 128), BF16)])
    return pl.pallas_call(
        functools.partial(fwd_kernel, slots, sp, rp),
        out_shape=[jax.ShapeDtypeStruct((docs, slots, width), BF16),
                   jax.ShapeDtypeStruct((docs, heads, rp, sp), BF16)],
        grid_spec=grid_spec, name="attend_forward",
        compiler_params=pltpu.CompilerParams(vmem_limit_bytes=56 << 20),
    )(lengths, qkv, qkv, qkv, relk, relq, boxes_col, boxes_row)


def bwd_kernel(slots, sp, rp, width, q_ref, k_ref, v_ref, dc_ref, p_ref, relk_ref, relq_ref, bc_ref, br_ref,
               dqkv_ref, gk_ref, gq_ref,
               qs, ks, dcs, base, ex, ey, vt, qt, kt, dct, mx, my, ds, dst, w2, o1, hs, dns, gs, gt, acc):
    pair = pl.program_id(1)
    nb = sp // 128
    tall = tall_block(rp)

    @pl.when(pair == 0)
    def _():
        for r in (qs, ks, dcs, ds, dst):
            r[...] = jnp.zeros_like(r)
        lane = iota((sp, 128), 1)
        ax = bc_ref[:, 0:1] >> 4
        ay = bc_ref[:, 1:2] >> 4
        left = lane < 64
        c = lane & 63
        a = jnp.where(left, ax, ay)
        one = jnp.where(c == a, 1.0, 0.0)
        nxt = jnp.where(c == a + 1, 1.0, 0.0)
        base[...] = one.astype(BF16)
        e = nxt - one
        ex[...] = jnp.where(left, e, 0.0).astype(BF16)
        ey[...] = jnp.where(left, 0.0, e).astype(BF16)

        def rows(b, c):
            r0 = at_block(b, 128)
            for t, m in ((0, mx), (1, my)):
                r_i = bc_ref[pl.ds(r0, 128), t:t + 1] & 15
                r_j = br_ref[t:t + 1, :] & 15
                m[pl.ds(r0, 128), :] = jnp.where(r_j >= r_i, 1.0, 0.0).astype(BF16)
            return c
        lax.fori_loop(0, nb, rows, 0)

    qs[0:slots, :] = v_ref[...]
    vt[...] = qs[...].T
    qs[0:slots, :] = q_ref[...]
    ks[0:slots, :] = k_ref[...]
    dcs[0:slots, :] = dc_ref[...]
    qt[...] = qs[...].T
    kt[...] = ks[...].T
    dct[...] = dcs[...].T

    def head(h, carry):
        mine = (iota((1, 128), 1) < 64) == (h == 0)
        mine_down = (iota((128, 1), 0) < 64) == (h == 0)

        def grad_scores(b, c):
            r0 = at_block(b, tall)
            d_b = jnp.where(mine, dcs[pl.ds(r0, tall), :], 0)
            dp = nn(d_b, vt[...])
            p = p_ref[h, pl.ds(r0, tall), :].astype(F32)
            inner = jnp.sum(p * dp, axis=1, keepdims=True)
            ds[pl.ds(r0, tall), 128:128 + sp] = (p * (dp - inner)).astype(BF16)
            return c
        each(rp // tall, grad_scores, True)

        def turn(b, c):
            r0 = at_block(b, 128)
            for jb in range(nb):
                dst[jb * 128:(jb + 1) * 128, pl.ds(r0 + 128, 128)] = \
                    ds[pl.ds(r0, 128), (jb + 1) * 128:(jb + 2) * 128].T
            return c
        each(nb, turn, True)

        dvt = nn(dct[:, 0:rp], p_ref[h, :, :])
        gt[...] = jnp.where(mine_down, dvt, gt[...])

        for side in range(2):
            mat = ds if side == 0 else dst
            other = ks if side == 0 else qs
            own_t = qt if side == 0 else kt
            rel_ref = relk_ref if side == 0 else relq_ref
            blk = iota((sp, 128), 0) >> 7
            lane_sp = iota((sp, 128), 1) & 63
            w2[:, 0:128] = jnp.where(mine, other[...].astype(F32), jnp.where(blk == lane_sp, 1.0, 0.0)).astype(BF16)
            w2[:, 128:256] = base[...]

            def spread(b, c):
                r0 = at_block(b, tall)
                d_b = mat[pl.ds(r0, tall), 128:128 + sp]
                out = nn(d_b, w2[...])
                o1[pl.ds(r0, tall), :] = out[:, :128]
                hs[pl.ds(r0, tall), :] = out[:, 128:] + nn(d_b * mx[pl.ds(r0, tall), :], ex[...]) \
                    + nn(d_b * my[pl.ds(r0, tall), :], ey[...])
                return c
            each(rp // tall, spread, True)

            def buckets(b, r0, n):
                lane = iota((n, 128), 1)
                row = iota((n, 128), 0)
                before = mat[pl.ds(r0, n), pl.ds(r0, 128)].astype(F32)
                here = mat[pl.ds(r0, n), pl.ds(r0 + 128, 128)].astype(F32)
                after = mat[pl.ds(r0, n), pl.ds(r0 + 256, 128)].astype(F32)
                sums = jnp.where(mine, 0.0, o1[pl.ds(r0, n), :])
                blkno = lane & 63
                low = jnp.where(blkno <= b - 2, sums, 0.0) + jnp.where(lane <= row + 64, before, 0.0) \
                    + jnp.where(lane <= row - 64, here, 0.0)
                high = jnp.where(blkno >= b + 2, sums, 0.0) + jnp.where(lane >= row + 63, here, 0.0) \
                    + jnp.where(lane >= row - 65, after, 0.0)
                ones = jnp.ones((256, 128), BF16)

                def across(part):
                    top = part.astype(BF16)
                    return nn(jnp.concatenate([top, (part - top.astype(F32)).astype(BF16)], axis=1), ones)
                low = across(low)
                high = across(high)
                near = jnp.where(lane >= row + 64, before, jnp.where(lane <= row - 65, after, here))
                mid = pick(near, (lane + row + 64) & 127)
                dn0 = jnp.where(lane == 0, low, jnp.where(lane == 127, high, mid))
                hist = hs[pl.ds(r0, n), :]
                c1 = lane + (bc_ref[pl.ds(r0, n), 0:1] >> 4) - 63
                c2 = lane + (bc_ref[pl.ds(r0, n), 1:2] >> 4) - 63
                dn1 = jnp.where((c1 >= 0) & (c1 < 64), pick(hist, c1 & 127), 0.0)
                dn2 = jnp.where((c2 >= 0) & (c2 < 64), pick(hist, (c2 + 64) & 127), 0.0)
                dns[pl.ds(r0, n), :] = jnp.concatenate([dn0, dn1, dn2], axis=1).astype(BF16)

            def bucket_block(b, c):
                buckets(b, at_block(b, 128), 128)
                return c
            each(rp // 128, bucket_block, True)
            if rp % 128:
                buckets(rp // 128, rp // 128 * 128, rp % 128)

            def gather_back(b, c):
                r0 = at_block(b, tall)
                g = (o1[pl.ds(r0, tall), :] + nn(dns[pl.ds(r0, tall), :], rel_ref[...])) * SCALE
                gs[side, pl.ds(r0, tall), :] = jnp.where(mine, g, gs[side, pl.ds(r0, tall), :].astype(F32)).astype(BF16)
                return c
            each(rp // tall, gather_back, True)
            acc[side] = jnp.where(mine_down, nn(own_t[:, 0:rp], dns[...]), acc[side])
        return carry
    lax.fori_loop(0, 2, head, 0)

    for side in range(2):
        dqkv_ref[:, pl.ds(pl.multiple_of(side * width + pair * 128, 128), 128)] = gs[side, 0:slots, :]
    gk_ref[...] = acc[0].T * SCALE
    gq_ref[...] = acc[1].T * SCALE
    dqkv_ref[:, pl.ds(pl.multiple_of(2 * width + pair * 128, 128), 128)] = gt[...].T[0:slots, :].astype(BF16)


def attend_backward(qkv, dctx, probs, relk, relq, boxes_col, boxes_row, heads):
    docs, slots, width = qkv.shape
    width = width // 3
    sp = boxes_row.shape[2]
    rp = -(-slots // 64) * 64
    pairs = heads // 2

    def part(t):
        return pl.BlockSpec((None, slots, 128), lambda d, p: (d, 0, t * pairs + p))
    rel = pl.BlockSpec((3 * BUCKETS, 128), lambda d, p: (0, p))
    grel = pl.BlockSpec((None, 3 * BUCKETS, 128), lambda d, p: (d, 0, p))
    return pl.pallas_call(
        functools.partial(bwd_kernel, slots, sp, rp, width),
        grid=(docs, pairs),
        in_specs=[part(0), part(1), part(2),
                  pl.BlockSpec((None, slots, 128), lambda d, p: (d, 0, p)),
                  pl.BlockSpec((None, 2, rp, sp), lambda d, p: (d, p, 0, 0)),
                  rel, rel,
                  pl.BlockSpec((None, sp, 2), lambda d, p: (d, 0, 0)),
                  pl.BlockSpec((None, 2, sp), lambda d, p: (d, 0, 0))],
        out_specs=[pl.BlockSpec((None, slots, 3 * width), lambda d, p: (d, 0, 0)), grel, grel],
        out_shape=[jax.ShapeDtypeStruct((docs, slots, 3 * width), BF16),
                   jax.ShapeDtypeStruct((docs, 3 * BUCKETS, width), F32),
                   jax.ShapeDtypeStruct((docs, 3 * BUCKETS, width), F32)],
        scratch_shapes=[pltpu.VMEM((sp, 128), BF16)] * 6 + [pltpu.VMEM((128, sp), BF16)] * 4
        + [pltpu.VMEM((sp, sp), BF16)] * 2 + [pltpu.VMEM((sp, sp + 256), BF16)] * 2
        + [pltpu.VMEM((sp, 256), BF16), pltpu.VMEM((rp, 128), F32), pltpu.VMEM((rp, 128), F32),
           pltpu.VMEM((rp, 384), BF16), pltpu.VMEM((2, rp, 128), BF16), pltpu.VMEM((128, sp), F32),
           pltpu.VMEM((2, 128, 384), F32)],
        name="attend_backward",
        compiler_params=pltpu.CompilerParams(vmem_limit_bytes=56 << 20),
    )(qkv, qkv, qkv, dctx, probs, relk, relq, boxes_col, boxes_row)


EPSILON = 1e-05
ROOT_HALF = math.sqrt(0.5)
PDF_SCALE = 1.0 / math.sqrt(2.0 * math.pi)


def dot_nt(a, b):
    return lax.dot_general(a, b, (((1,), (1,)), ((), ())), preferred_element_type=F32)


def dot_tn(a, b):
    return lax.dot_general(a, b, (((0,), (0,)), ((), ())), preferred_element_type=F32)


def norm_rows(values, gain, shift):
    mean = jnp.mean(values, axis=1, keepdims=True)
    scale = lax.rsqrt(jnp.mean(values * values, axis=1, keepdims=True) - mean * mean + EPSILON)
    unit = (values - mean) * scale
    return unit * gain + shift, unit, scale


def norm_pull(upstream, unit, scale, gain):
    scaled = upstream * gain
    first = jnp.mean(scaled, axis=1, keepdims=True)
    second = jnp.mean(scaled * unit, axis=1, keepdims=True)
    return scale * (scaled - first - unit * second)


def exchange_sum(parts, bits, size, beside):
    place = lax.axis_index("dp")

    def swap(array, bit):
        return lax.ppermute(array, "dp", [(i, i ^ bit) for i in range(size)])

    def fold(array, bit):
        half = array.shape[0] // 2
        low = (place & bit) == 0
        keep = jnp.where(low, array[:half], array[half:])
        send = jnp.where(low, array[half:], array[:half])
        return (keep.astype(F32) + swap(send, bit).astype(F32)).astype(BF16)

    def unfold(array, bit):
        low = (place & bit) == 0
        other = swap(array, bit)
        return jnp.concatenate([jnp.where(low, array, other), jnp.where(low, other, array)], axis=0)

    arrays = [a for a, _ in parts]
    for step in range(len(bits)):
        arrays = [fold(a, order[step]) for a, (_, order) in zip(arrays, parts)]
    for step in reversed(range(len(bits))):
        if step == 0:
            arrays, beside = lax.optimization_barrier((arrays, beside))
        arrays = [unfold(a, order[step]) for a, (_, order) in zip(arrays, parts)]
    return arrays, beside


def sum_over_documents(table, size, beside):
    if size != 16:
        return lax.psum(table, "dp"), beside
    rows = table.shape[0]
    grain = 256
    pieces = 4
    step = -(-rows // (pieces * grain)) * grain
    padded = jnp.pad(table, ((0, pieces * step - rows), (0, 0)))
    orders = ((1, 2, 4, 8), (1, 4, 2, 8))
    parts = [(padded[i * step:(i + 1) * step], orders[i % 2]) for i in range(pieces)]
    arrays, beside = exchange_sum(parts, orders[0], size, beside)
    return jnp.concatenate(arrays, axis=0)[:rows], beside


def on_device(
    documents,
    shards,
    hidden_in,
    lengths,
    boxes,
    w_qkv,
    w_out,
    w_up,
    w_down,
    rel_keys,
    rel_queries,
    norm_gains,
    norm_shifts,
    out_grad,
):
    doc_count, slot_count, width = hidden_in.shape
    row_count = doc_count * slot_count
    model_width = w_qkv.shape[0]
    heads_here = width // HEAD_DIM
    me = lax.axis_index("tensor")
    pair = [(0, 1), (1, 0)]

    def join(array, axis):
        if shards != 2:
            return lax.all_gather(array, "tensor", axis=axis, tiled=True)
        other = lax.ppermute(array, "tensor", pair)
        first = me == 0
        return jnp.concatenate(
            [jnp.where(first, array, other), jnp.where(first, other, array)], axis=axis)

    def total(partial):
        if shards != 2:
            return lax.psum(partial, "tensor").astype(F32)
        return partial.astype(F32) + lax.ppermute(partial, "tensor", pair).astype(F32)

    def own(array):
        return lax.dynamic_slice_in_dim(array, me * width, width, axis=array.ndim - 1)

    def own_total(partial):
        if shards != 2:
            return lax.psum_scatter(partial, "tensor", scatter_dimension=1, tiled=True).astype(F32)
        send = lax.dynamic_slice_in_dim(partial, (1 - me) * width, width, axis=1)
        return own(partial).astype(F32) + lax.ppermute(send, "tensor", pair).astype(F32)

    rel_k = rel_keys.reshape(3 * BUCKETS, width)
    rel_q = rel_queries.reshape(3 * BUCKETS, width)
    padded = -(-slot_count // 128) * 128
    boxes_col = jnp.pad(boxes, ((0, 0), (0, padded - slot_count), (0, 0)))
    boxes_row = jnp.swapaxes(boxes_col, 1, 2)

    rows = join(hidden_in.reshape(row_count, width), 1)
    weight_qkv = w_qkv.reshape(model_width, 3 * width)
    projected = jnp.dot(rows, weight_qkv, preferred_element_type=F32).astype(BF16)
    norms = join(jnp.concatenate([norm_gains, norm_shifts], axis=0), 1)
    rows, out_rows = lax.optimization_barrier((rows, out_grad.reshape(row_count, width)))
    upstream = join(out_rows, 1)
    out_whole = join(w_out, 0)
    projected = projected.reshape(doc_count, slot_count, 3 * width)
    context, probs = attend_forward(lengths, projected, rel_k.T, rel_q.T, boxes_col, boxes_row, heads_here)
    context, upstream, norms, out_whole = lax.optimization_barrier((context, upstream, norms, out_whole))
    context = context.reshape(row_count, width)

    middle = row_count // 2 // 32 * 32 + 32 if row_count > 64 else row_count
    spans = [(a, b) for a, b in ((0, middle), (middle, row_count)) if b > a]
    join_context = [join(context[a:b], 1) for a, b in spans]
    first = []
    for (a, b), whole in zip(spans, join_context):
        attn = jnp.dot(whole, out_whole, preferred_element_type=F32)
        h1, unit, scale = norm_rows(rows[a:b].astype(F32) + attn, norms[0:1], norms[2:3])
        low = h1.astype(BF16)
        upper = jnp.dot(low, w_up, preferred_element_type=F32)
        chance = 0.5 * (1.0 + lax.erf(upper * ROOT_HALF))
        active = (upper * chance).astype(BF16)
        slope = (chance + upper * (PDF_SCALE * jnp.exp(-0.5 * upper * upper))).astype(BF16)
        ffn = total(jnp.dot(active, w_down, preferred_element_type=F32).astype(BF16))
        first.append((h1, unit, scale, low, active, slope, ffn))
    second = []
    for (a, b), (h1, unit, scale, low, active, slope, ffn) in zip(spans, first):
        result, unit_second, scale_second = norm_rows(h1 + ffn, norms[1:2], norms[3:4])
        up = upstream[a:b].astype(F32)
        grad = norm_pull(up, unit_second, scale_second, norms[1:2])
        grad, ffn_grad = lax.optimization_barrier((grad, grad.astype(BF16)))
        grad_upper = (dot_nt(ffn_grad, w_down) * slope.astype(F32)).astype(BF16)
        hidden = total(dot_nt(grad_upper, w_up).astype(BF16))
        sums = jnp.stack([jnp.sum(up * unit_second, axis=0), jnp.sum(up, axis=0)])
        second.append((result, grad, ffn_grad, grad_upper, hidden, sums))
    def stacked(found):
        return jnp.concatenate(found, axis=0)

    hidden_out = own(stacked([f[0].astype(BF16) for f in second])).reshape(doc_count, slot_count, width)
    hidden_out, arrived = lax.optimization_barrier((hidden_out, second[-1][4]))
    second[-1] = second[-1][:4] + (arrived,) + second[-1][5:]
    third = []
    for (h1, unit, scale, low, active, slope, ffn), (result, grad, ffn_grad, grad_upper, hidden, sums) in zip(first, second):
        grad_hidden = grad + hidden
        pulled = norm_pull(grad_hidden, unit, scale, norms[0:1])
        mine = jnp.stack([jnp.sum(grad_hidden * unit, axis=0), jnp.sum(grad_hidden, axis=0)])
        third.append((pulled, mine))

    ffn_grad = stacked([f[2] for f in second])
    grad_upper = stacked([f[3] for f in second])
    h1_low = stacked([f[3] for f in first])
    down_grad = dot_tn(stacked([f[4] for f in first]), ffn_grad).astype(BF16)
    up_grad = dot_tn(h1_low, grad_upper).astype(BF16)
    ffn_sums = lax.psum((down_grad, up_grad), "dp")
    grad_first = stacked([f[0] for f in third])
    attn_grad = grad_first.astype(BF16)
    sums_second = sum(f[5] for f in second)
    sums_first = sum(f[1] for f in third)
    norm_grads = own(jnp.stack([sums_first[0], sums_second[0], sums_first[1], sums_second[1]]))

    out_weight_grad = dot_tn(context, attn_grad)
    grad_context = dot_nt(attn_grad, w_out).astype(BF16).reshape(doc_count, slot_count, width)
    grad_projected, rel_k_sum, rel_q_sum = attend_backward(
        projected, grad_context, probs, rel_k, rel_q, boxes_col, boxes_row, heads_here
    )
    grad_rows = grad_projected.reshape(row_count, 3 * width)
    input_part = dot_nt(grad_rows, weight_qkv).astype(BF16)
    input_grad = own(grad_first) + own_total(input_part)
    input_grad = input_grad.astype(BF16).reshape(doc_count, slot_count, width)
    qkv_grads = [dot_tn(rows, grad_rows[:, t * width:(t + 1) * width]) for t in range(3)]
    pieces = qkv_grads + [jnp.sum(rel_k_sum, axis=0), jnp.sum(rel_q_sum, axis=0)]
    pieces += [out_weight_grad[:, t * width:(t + 1) * width] for t in range(shards)]
    pieces += [norm_grads]
    table, (down_grad, up_grad) = sum_over_documents(
        jnp.concatenate([p.astype(BF16) for p in pieces], axis=0), documents, ffn_sums)
    table = table.astype(F32)
    found = []
    at = 0
    for p in pieces:
        found.append(table[at:at + p.shape[0]])
        at += p.shape[0]
    qkv_grad = jnp.stack(found[0:3], axis=1)
    rel_keys_grad = found[3].reshape(3, BUCKETS, width)
    rel_queries_grad = found[4].reshape(3, BUCKETS, width)
    out_weight_grad = jnp.concatenate(found[5:5 + shards], axis=1)
    norm_grads = found[5 + shards]
    return (
        hidden_out,
        input_grad,
        qkv_grad,
        out_weight_grad,
        up_grad.astype(F32),
        down_grad.astype(F32),
        rel_keys_grad,
        rel_queries_grad,
        norm_grads[0:2],
        norm_grads[2:4],
    )


def solution(mesh):
    in_specs = (
        P("dp", None, "tensor"),
        P("dp"),
        P("dp", None, None),
        P(None, None, "tensor"),
        P("tensor", None),
        P(None, "tensor"),
        P("tensor", None),
        P(None, None, "tensor"),
        P(None, None, "tensor"),
        P(None, "tensor"),
        P(None, "tensor"),
        P("dp", None, "tensor"),
    )
    out_specs = (
        P("dp", None, "tensor"),
        P("dp", None, "tensor"),
        P(None, None, "tensor"),
        P("tensor", None),
        P(None, "tensor"),
        P("tensor", None),
        P(None, None, "tensor"),
        P(None, None, "tensor"),
        P(None, "tensor"),
        P(None, "tensor"),
    )
    body = functools.partial(on_device, mesh.shape["dp"], mesh.shape["tensor"])
    return jax.shard_map(body, mesh=mesh, in_specs=in_specs, out_specs=out_specs, check_vma=False)
```

profile of v0, /device:TPU:0, one launch (start us, length us, event | category | flops | bytes accessed | tf_op | source)
XLA Modules:
  0.0 380.3 jit_solution(331551769694727814)
XLA Ops:
  7.2 3.1 collective-permute-start
  19.5 3.2 copy.26
  29.1 3.2 fusion.q_ref.k_ref.v_ref
  32.3 40.4 %attend_forward.1 = (bf16[1,561,512]{2,1,0:T(8,128)(2,1)}, bf16[1,8,576,640]{3,2,1,0:T(8,128)(2,1)}) custom-call(s32[1]{0:T(128)S(6)} %copy.48.len_ref, bf16[1,561,1536]{2,1,0:T(8,128)(2,1)} %fusion.q_ref.k_ref.v_ref, bf16[1,561,1536]{2,1,0:T(8,128)(2,1)} %fusion.q_ref.k_ref.v_ref, bf16[1,561,1536]{2,1,0:T(8,128)(2,1)} %fusion.q_ref.k_ref.v_ref, ...), custom_call_target="tpu_custom_call" | custom-call | tf_op jit(solution)/shard_map/attend_forward/pallas_call | solution.py:207
  77.7 7.4 %collective-permute-done.6 = bf16[273,512]{1,0:T(8,128)(2,1)S(1)} collective-permute-done((bf16[273,512]{1,0:T(8,128)(2,1)S(1)}, bf16[273,512]{1,0:T(8,128)(2,1)S(1)}, u32[]{:S(2)}, u32[]{:S(2)}) %collective-permute-start.6) | collective-permute-done | bytes 279584 | tf_op jit(solution)/shard_map/ppermute | solution.py:485
  97.7 9.3 %collective-permute-done.7 = bf16[273,1024]{1,0:T(8,128)(2,1)S(1)} collective-permute-done((bf16[273,1024]{1,0:T(8,128)(2,1)S(1)}, bf16[273,1024]{1,0:T(8,128)(2,1)S(1)}, u32[]{:S(2)}, u32[]{:S(2)}) %collective-permute-start.7) | collective-permute-done | bytes 559136 | tf_op jit(solution)/shard_map/ppermute | solution.py:493
  109.8 2.4 fusion.2
  114.6 4.8 %collective-permute-done.5 = bf16[288,1024]{1,0:T(8,128)(2,1)S(1)} collective-permute-done((bf16[288,1024]{1,0:T(8,128)(2,1)S(1)}, bf16[288,1024]{1,0:T(8,128)(2,1)S(1)}, u32[]{:S(2)}, u32[]{:S(2)}) %collective-permute-start.5) | collective-permute-done | bytes 589856 | tf_op jit(solution)/shard_map/ppermute | solution.py:493
  126.5 5.0 %convolution_convert_fusion = bf16[1024,2048]{1,0:T(8,128)(2,1)} fusion(bf16[273,2048]{1,0:T(8,128)(2,1)S(1)} %fusion.2, bf16[288,2048]{1,0:T(8,128)(2,1)S(1)} %fusion.1, bf16[273,1024]{1,0:T(8,128)(2,1)S(1)} %fusion.45, bf16[288,1024]{1,0:T(8,128)(2,1)S(1)} %fusion.44), kind=kOutput, calls=%fused_computation.3 | convolution fusion | flops 2361995264 | bytes 7641088 | tf_op jit(solution)/shard_map/dot_general | solution.py:400
  131.5 5.5 %convolution_convert_fusion.1 = bf16[2048,1024]{1,0:T(8,128)(2,1)} fusion(bf16[273,2048]{1,0:T(8,128)(2,1)S(1)} %get-tuple-element.171, bf16[288,2048]{1,0:T(8,128)(2,1)S(1)} %get-tuple-element.168, bf16[273,1024]{1,0:T(8,128)(2,1)S(1)} %get-tuple-element.40, bf16[288,1024]{1,0:T(8,128)(2,1)S(1)} %get-tuple-element.43), kind=kOutput, calls=%fused_computation.4 | convolution fusion | flops 2361995264 | bytes 7641088 | tf_op jit(solution)/shard_map/dot_general | solution.py:400
  142.0 5.3 %collective-permute-done.9 = bf16[288,1024]{1,0:T(8,128)(2,1)} collective-permute-done((bf16[288,1024]{1,0:T(8,128)(2,1)}, bf16[288,1024]{1,0:T(8,128)(2,1)}, u32[]{:S(2)}, u32[]{:S(2)}) %collective-permute-start.9) | collective-permute-done | bytes 589856 | tf_op jit(solution)/shard_map/ppermute | solution.py:493
  153.4 32.9 %attend_backward.1 = (bf16[1,561,1536]{2,1,0:T(8,128)(2,1)}, f32[1,384,512]{2,1,0:T(8,128)}, f32[1,384,512]{2,1,0:T(8,128)}) custom-call(bf16[1,561,1536]{2,1,0:T(8,128)(2,1)} %fusion.q_ref.k_ref.v_ref, bf16[1,561,1536]{2,1,0:T(8,128)(2,1)} %fusion.q_ref.k_ref.v_ref, bf16[1,561,1536]{2,1,0:T(8,128)(2,1)} %fusion.q_ref.k_ref.v_ref, ...), custom_call_target="tpu_custom_call" | custom-call | tf_op jit(solution)/shard_map/attend_backward/pallas_call | solution.py:367
  202.8 6.2 %collective-permute-done.33 = bf16[320,512]{1,0:T(8,128)(2,1)S(1)} collective-permute-done((bf16[320,512]{1,0:T(8,128)(2,1)S(1)}, bf16[320,512]{1,0:T(8,128)(2,1)S(1)}, u32[]{:S(2)}, u32[]{:S(2)}) %collective-permute-start.33) | collective-permute-done | bytes 327712 | tf_op jit(solution)/shard_map/ppermute | solution.py:421
  210.5 9.6 %collective-permute-done.19 = bf16[320,512]{1,0:T(8,128)(2,1)S(1)} collective-permute-done((bf16[320,512]{1,0:T(8,128)(2,1)S(1)}, bf16[320,512]{1,0:T(8,128)(2,1)S(1)}, u32[]{:S(2)}, u32[]{:S(2)}) %collective-permute-start.19) | collective-permute-done | bytes 327712 | tf_op jit(solution)/shard_map/ppermute | solution.py:421
  229.2 2.9 collective-permute-start.35
  234.3 2.9 collective-permute-done.27
  237.3 3.2 collective-permute-done.13
  240.7 3.0 collective-permute-start.36
  243.7 4.1 %collective-permute-done.21 = bf16[80,512]{1,0:T(8,128)(2,1)S(1)} collective-permute-done((bf16[80,512]{1,0:T(8,128)(2,1)S(1)}, bf16[80,512]{1,0:T(8,128)(2,1)S(1)}, u32[]{:S(2)}, u32[]{:S(2)}) %collective-permute-start.21) | collective-permute-done | bytes 81952 | tf_op jit(solution)/shard_map/ppermute | solution.py:421
  247.9 6.4 %collective-permute-done.28 = bf16[80,512]{1,0:T(8,128)(2,1)S(1)} collective-permute-done((bf16[80,512]{1,0:T(8,128)(2,1)S(1)}, bf16[80,512]{1,0:T(8,128)(2,1)S(1)}, u32[]{:S(2)}, u32[]{:S(2)}) %collective-permute-start.28) | collective-permute-done | bytes 81952 | tf_op jit(solution)/shard_map/ppermute | solution.py:421
  254.4 3.9 %collective-permute-done.14 = bf16[80,512]{1,0:T(8,128)(2,1)S(1)} collective-permute-done((bf16[80,512]{1,0:T(8,128)(2,1)S(1)}, bf16[80,512]{1,0:T(8,128)(2,1)S(1)}, u32[]{:S(2)}, u32[]{:S(2)}) %collective-permute-start.14) | collective-permute-done | bytes 81952 | tf_op jit(solution)/shard_map/ppermute | solution.py:421
  258.4 7.1 %collective-permute-done.36 = bf16[80,512]{1,0:T(8,128)(2,1)S(1)} collective-permute-done((bf16[80,512]{1,0:T(8,128)(2,1)S(1)}, bf16[80,512]{1,0:T(8,128)(2,1)S(1)}, u32[]{:S(2)}, u32[]{:S(2)}) %collective-permute-start.36) | collective-permute-done | bytes 81952 | tf_op jit(solution)/shard_map/ppermute | solution.py:421
  267.0 2.7 collective-permute-done.22
  277.8 4.7 %collective-permute-done.30 = bf16[160,512]{1,0:T(8,128)(2,1)S(1)} collective-permute-done((bf16[160,512]{1,0:T(8,128)(2,1)S(1)}, bf16[160,512]{1,0:T(8,128)(2,1)S(1)}, u32[]{:S(2)}, u32[]{:S(2)}) %collective-permute-start.30) | collective-permute-done | bytes 163872 | tf_op jit(solution)/shard_map/ppermute | solution.py:421
  282.6 6.9 %collective-permute-done.16 = bf16[160,512]{1,0:T(8,128)(2,1)S(1)} collective-permute-done((bf16[160,512]{1,0:T(8,128)(2,1)S(1)}, bf16[160,512]{1,0:T(8,128)(2,1)S(1)}, u32[]{:S(2)}, u32[]{:S(2)}) %collective-permute-start.16) | collective-permute-done | bytes 163872 | tf_op jit(solution)/shard_map/ppermute | solution.py:421
  289.6 13.9 %collective-permute-done.38 = bf16[320,512]{1,0:T(8,128)(2,1)S(1)} collective-permute-done((bf16[320,512]{1,0:T(8,128)(2,1)S(1)}, bf16[320,512]{1,0:T(8,128)(2,1)S(1)}, u32[]{:S(2)}, u32[]{:S(2)}) %collective-permute-start.38) | collective-permute-done | bytes 327712 | tf_op jit(solution)/shard_map/ppermute | solution.py:421
  303.6 11.2 %collective-permute-done.24 = bf16[320,512]{1,0:T(8,128)(2,1)S(1)} collective-permute-done((bf16[320,512]{1,0:T(8,128)(2,1)S(1)}, bf16[320,512]{1,0:T(8,128)(2,1)S(1)}, u32[]{:S(2)}, u32[]{:S(2)}) %collective-permute-start.24) | collective-permute-done | bytes 327712 | tf_op jit(solution)/shard_map/ppermute | solution.py:421
  315.4 32.2 %all-reduce.5.cloned.1.call-done = (bf16[2048,1024]{1,0:T(8,128)(2,1)}, bf16[1024,2048]{1,0:T(8,128)(2,1)}) async-done(((bf16[2048,1024]{1,0:T(8,128)(2,1)}, bf16[1024,2048]{1,0:T(8,128)(2,1)}), (bf16[2048,1024]{1,0:T(8,128)(2,1)}, bf16[1024,2048]{1,0:T(8,128)(2,1)})) %all-reduce.5.cloned.1.call-update) | async-done | bytes 8388624 | tf_op jit(solution)/shard_map/psum | solution.py:564
  348.1 2.6 fusion.55
  351.3 6.8 %convert_element_type.394 = f32[1024,2048]{1,0:T(8,128)} convert(bf16[1024,2048]{1,0:T(8,128)(2,1)} %get-tuple-element.54) | non-fusion elementwise | flops 2097152 | bytes 12582912 | tf_op jit(solution)/shard_map/convert_element_type | solution.py:602
  358.1 4.6 %convert_element_type.395 = f32[2048,1024]{1,0:T(8,128)} convert(bf16[2048,1024]{1,0:T(8,128)(2,1)S(1)} %copy-done.3) | non-fusion elementwise | flops 2097152 | bytes 12582912 | tf_op jit(solution)/shard_map/convert_element_type | solution.py:603
  369.9 3.4 pad_maximum_fusion
  (250 shorter events, 103.8 us)
Async XLA Ops:
  7.2 340.4 %all-reduce.5.cloned.1.call-start = ((), (), s32[]{:S(2)}) async-start(), calls=%async_computation | async-start | bytes 16777216 | tf_op jit(solution)/shard_map/psum | solution.py:564
  7.2 17.5 %collective-permute-start = (bf16[561,512]{1,0:T(8,128)(2,1)}, bf16[561,512]{1,0:T(8,128)(2,1)}, u32[]{:S(2)}, u32[]{:S(2)}) collective-permute-start(bf16[561,512]{1,0:T(8,128)(2,1)} %bitcast.97), channel_id=1, source_target_pairs={{0,1},{1,0},{2,3},{3,2},{4,5},{5,4},{6,7},{7,6},{8,9},{9,8},{10,11... | collective-permute-start | bytes 1723400 | tf_op jit(solution)/shard_map/ppermute | solution.py:485
  11.0 13.7 %collective-permute-start.2 = (f32[4,512]{1,0:T(4,128)S(1)}, f32[4,512]{1,0:T(4,128)S(1)}, u32[]{:S(2)}, u32[]{:S(2)}) collective-permute-start(f32[4,512]{1,0:T(4,128)S(1)} %pad_maximum_fusion.24), channel_id=1, source_target_pairs={{0,1},{1,0},{2,3},{3,2},{4,5},{5,4},{6,7},{7,6},{8,9},{9,8},{10,11... | collective-permute-start | bytes 24584 | tf_op jit(solution)/shard_map/ppermute | solution.py:485
  11.1 61.7 %collective-permute-start.3 = (bf16[512,1024]{1,0:T(8,128)(2,1)}, bf16[512,1024]{1,0:T(8,128)(2,1)}, u32[]{:S(2)}, u32[]{:S(2)}) collective-permute-start(bf16[512,1024]{1,0:T(8,128)(2,1)} %param.16), channel_id=1, source_target_pairs={{0,1},{1,0},{2,3},{3,2},{4,5},{5,4},{6,7},{7,6},{8,9},{9,8},{10,11... | collective-permute-start | bytes 3145736 | tf_op jit(solution)/shard_map/ppermute | solution.py:485
  27.1 47.2 %collective-permute-start.1 = (bf16[561,512]{1,0:T(8,128)(2,1)S(1)}, bf16[561,512]{1,0:T(8,128)(2,1)S(1)}, u32[]{:S(2)}, u32[]{:S(2)}) collective-permute-start(bf16[561,512]{1,0:T(8,128)(2,1)S(1)} %bitcast.98), channel_id=1, source_target_pairs={{0,1},{1,0},{2,3},{3,2},{4,5},{5,4},{6,7},{7,6},{8,9},{9,8},{10,11... | collective-permute-start | bytes 1723400 | tf_op jit(solution)/shard_map/ppermute | solution.py:485
  75.6 15.6 %collective-permute-start.4 = (bf16[288,512]{1,0:T(8,128)(2,1)S(1)}, bf16[288,512]{1,0:T(8,128)(2,1)S(1)}, u32[]{:S(2)}, u32[]{:S(2)}) collective-permute-start(bf16[288,512]{1,0:T(8,128)(2,1)S(1)} %slice_bitcast_fusion.3), channel_id=1, source_target_pairs={{0,1},{1,0},{2,3},{3,2},{4,5},{5,4},{6,7},{7,6},{8,9},{9,8},{10,11... | collective-permute-start | bytes 884744 | tf_op jit(solution)/shard_map/ppermute | solution.py:485
  91.0 15.9 %collective-permute-start.7 = (bf16[273,1024]{1,0:T(8,128)(2,1)S(1)}, bf16[273,1024]{1,0:T(8,128)(2,1)S(1)}, u32[]{:S(2)}, u32[]{:S(2)}) collective-permute-start(bf16[273,1024]{1,0:T(8,128)(2,1)S(1)} %convolution_convert_fusion.12), channel_id=1, source_target_pairs={{0,1},{1,0},{2,3},{3,2},{4,5},{5,4},{6,7},{7,6},{8,9},{9,8},{10,11... | collective-permute-start | bytes 1677320 | tf_op jit(solution)/shard_map/ppermute | solution.py:493
  95.7 23.7 %collective-permute-start.5 = (bf16[288,1024]{1,0:T(8,128)(2,1)S(1)}, bf16[288,1024]{1,0:T(8,128)(2,1)S(1)}, u32[]{:S(2)}, u32[]{:S(2)}) collective-permute-start(bf16[288,1024]{1,0:T(8,128)(2,1)S(1)} %convolution_convert_fusion.9), channel_id=1, source_target_pairs={{0,1},{1,0},{2,3},{3,2},{4,5},{5,4},{6,7},{7,6},{8,9},{9,8},{10,11... | collective-permute-start | bytes 1769480 | tf_op jit(solution)/shard_map/ppermute | solution.py:493
  114.5 24.9 %collective-permute-start.8 = (bf16[273,1024]{1,0:T(8,128)(2,1)}, bf16[273,1024]{1,0:T(8,128)(2,1)}, u32[]{:S(2)}, u32[]{:S(2)}) collective-permute-start(bf16[273,1024]{1,0:T(8,128)(2,1)} %convolution_convert_fusion.11), channel_id=1, source_target_pairs={{0,1},{1,0},{2,3},{3,2},{4,5},{5,4},{6,7},{7,6},{8,9},{9,8},{10,11... | collective-permute-start | bytes 1677320 | tf_op jit(solution)/shard_map/ppermute | solution.py:493
  196.4 151.7 %collective-permute-start.10 = (bf16[561,512]{1,0:T(8,128)(2,1)S(1)}, bf16[561,512]{1,0:T(8,128)(2,1)}, u32[]{:S(2)}, u32[]{:S(2)}) collective-permute-start(bf16[561,512]{1,0:T(8,128)(2,1)S(1)} %constant_dynamic-slice_fusion), channel_id=1, source_target_pairs={{0,1},{1,0},{2,3},{3,2},{4,5},{5,4},{6,7},{7,6},{8,9},{9,8},{10,11... | collective-permute-start | bytes 1723400 | tf_op jit(solution)/shard_map/ppermute | solution.py:502
  199.7 20.4 %collective-permute-start.19 = (bf16[320,512]{1,0:T(8,128)(2,1)S(1)}, bf16[320,512]{1,0:T(8,128)(2,1)S(1)}, u32[]{:S(2)}, u32[]{:S(2)}) collective-permute-start(bf16[320,512]{1,0:T(8,128)(2,1)S(1)} %broadcast_select_fusion.15), channel_id=1, source_target_pairs={{0,8},{2,10},{4,12},{6,14},{8,0},{10,2},{12,4},{14,6},{16,24},{18,... | collective-permute-start | bytes 983048 | tf_op jit(solution)/shard_map/ppermute | solution.py:421
  200.3 21.9 %collective-permute-start.26 = (bf16[320,512]{1,0:T(8,128)(2,1)S(1)}, bf16[320,512]{1,0:T(8,128)(2,1)S(1)}, u32[]{:S(2)}, u32[]{:S(2)}) collective-permute-start(bf16[320,512]{1,0:T(8,128)(2,1)S(1)} %broadcast_select_fusion.18), channel_id=1, source_target_pairs={{0,4},{2,6},{4,0},{6,2},{8,12},{10,14},{12,8},{14,10},{16,20},{18,... | collective-permute-start | bytes 983048 | tf_op jit(solution)/shard_map/ppermute | solution.py:421
  202.4 23.1 %collective-permute-start.12 = (bf16[320,512]{1,0:T(8,128)(2,1)S(1)}, bf16[320,512]{1,0:T(8,128)(2,1)S(1)}, u32[]{:S(2)}, u32[]{:S(2)}) collective-permute-start(bf16[320,512]{1,0:T(8,128)(2,1)S(1)} %broadcast_select_fusion.21), channel_id=1, source_target_pairs={{0,4},{2,6},{4,0},{6,2},{8,12},{10,14},{12,8},{14,10},{16,20},{18,... | collective-permute-start | bytes 983048 | tf_op jit(solution)/shard_map/ppermute | solution.py:421
  209.2 19.9 %collective-permute-start.34 = (bf16[160,512]{1,0:T(8,128)(2,1)S(1)}, bf16[160,512]{1,0:T(8,128)(2,1)S(1)}, u32[]{:S(2)}, u32[]{:S(2)}) collective-permute-start(bf16[160,512]{1,0:T(8,128)(2,1)S(1)} %broadcast_select_fusion.28), channel_id=1, source_target_pairs={{0,4},{2,6},{4,0},{6,2},{8,12},{10,14},{12,8},{14,10},{16,20},{18,... | collective-permute-start | bytes 491528 | tf_op jit(solution)/shard_map/ppermute | solution.py:421
  222.4 14.8 %collective-permute-start.27 = (bf16[160,512]{1,0:T(8,128)(2,1)S(1)}, bf16[160,512]{1,0:T(8,128)(2,1)S(1)}, u32[]{:S(2)}, u32[]{:S(2)}) collective-permute-start(bf16[160,512]{1,0:T(8,128)(2,1)S(1)} %broadcast_select_fusion.34), channel_id=1, source_target_pairs={{0,8},{2,10},{4,12},{6,14},{8,0},{10,2},{12,4},{14,6},{16,24},{18,... | collective-permute-start | bytes 491528 | tf_op jit(solution)/shard_map/ppermute | solution.py:421
  225.7 14.8 %collective-permute-start.13 = (bf16[160,512]{1,0:T(8,128)(2,1)S(1)}, bf16[160,512]{1,0:T(8,128)(2,1)S(1)}, u32[]{:S(2)}, u32[]{:S(2)}) collective-permute-start(bf16[160,512]{1,0:T(8,128)(2,1)S(1)} %broadcast_select_fusion.37), channel_id=1, source_target_pairs={{0,8},{2,10},{4,12},{6,14},{8,0},{10,2},{12,4},{14,6},{16,24},{18,... | collective-permute-start | bytes 491528 | tf_op jit(solution)/shard_map/ppermute | solution.py:421
  232.1 15.7 %collective-permute-start.21 = (bf16[80,512]{1,0:T(8,128)(2,1)S(1)}, bf16[80,512]{1,0:T(8,128)(2,1)S(1)}, u32[]{:S(2)}, u32[]{:S(2)}) collective-permute-start(bf16[80,512]{1,0:T(8,128)(2,1)S(1)} %broadcast_select_fusion.46), channel_id=1, source_target_pairs={{0,16},{2,18},{4,20},{6,22},{8,24},{10,26},{12,28},{14,30},{16,0},... | collective-permute-start | bytes 245768 | tf_op jit(solution)/shard_map/ppermute | solution.py:421
  237.2 17.0 %collective-permute-start.28 = (bf16[80,512]{1,0:T(8,128)(2,1)S(1)}, bf16[80,512]{1,0:T(8,128)(2,1)S(1)}, u32[]{:S(2)}, u32[]{:S(2)}) collective-permute-start(bf16[80,512]{1,0:T(8,128)(2,1)S(1)} %broadcast_select_fusion.43), channel_id=1, source_target_pairs={{0,16},{2,18},{4,20},{6,22},{8,24},{10,26},{12,28},{14,30},{16,0},... | collective-permute-start | bytes 245768 | tf_op jit(solution)/shard_map/ppermute | solution.py:421
  240.6 17.7 %collective-permute-start.14 = (bf16[80,512]{1,0:T(8,128)(2,1)S(1)}, bf16[80,512]{1,0:T(8,128)(2,1)S(1)}, u32[]{:S(2)}, u32[]{:S(2)}) collective-permute-start(bf16[80,512]{1,0:T(8,128)(2,1)S(1)} %broadcast_select_fusion.49), channel_id=1, source_target_pairs={{0,16},{2,18},{4,20},{6,22},{8,24},{10,26},{12,28},{14,30},{16,0},... | collective-permute-start | bytes 245768 | tf_op jit(solution)/shard_map/ppermute | solution.py:421
  240.7 24.7 %collective-permute-start.36 = (bf16[80,512]{1,0:T(8,128)(2,1)S(1)}, bf16[80,512]{1,0:T(8,128)(2,1)S(1)}, u32[]{:S(2)}, u32[]{:S(2)}) collective-permute-start(bf16[80,512]{1,0:T(8,128)(2,1)S(1)} %add_convert_fusion.14), channel_id=1, source_target_pairs={{0,16},{2,18},{4,20},{6,22},{8,24},{10,26},{12,28},{14,30},{16,0},... | collective-permute-start | bytes 245768 | tf_op jit(solution)/shard_map/ppermute | solution.py:421
  247.8 21.8 %collective-permute-start.22 = (bf16[80,512]{1,0:T(8,128)(2,1)S(1)}, bf16[80,512]{1,0:T(8,128)(2,1)S(1)}, u32[]{:S(2)}, u32[]{:S(2)}) collective-permute-start(bf16[80,512]{1,0:T(8,128)(2,1)S(1)} %add_convert_fusion.16), channel_id=1, source_target_pairs={{0,16},{2,18},{4,20},{6,22},{8,24},{10,26},{12,28},{14,30},{16,0},... | collective-permute-start | bytes 245768 | tf_op jit(solution)/shard_map/ppermute | solution.py:421
  254.3 18.0 %collective-permute-start.29 = (bf16[80,512]{1,0:T(8,128)(2,1)S(1)}, bf16[80,512]{1,0:T(8,128)(2,1)S(1)}, u32[]{:S(2)}, u32[]{:S(2)}) collective-permute-start(bf16[80,512]{1,0:T(8,128)(2,1)S(1)} %add_convert_fusion.15), channel_id=1, source_target_pairs={{0,16},{2,18},{4,20},{6,22},{8,24},{10,26},{12,28},{14,30},{16,0},... | collective-permute-start | bytes 245768 | tf_op jit(solution)/shard_map/ppermute | solution.py:421
  258.3 14.9 %collective-permute-start.15 = (bf16[80,512]{1,0:T(8,128)(2,1)S(1)}, bf16[80,512]{1,0:T(8,128)(2,1)S(1)}, u32[]{:S(2)}, u32[]{:S(2)}) collective-permute-start(bf16[80,512]{1,0:T(8,128)(2,1)S(1)} %add_convert_fusion.17), channel_id=1, source_target_pairs={{0,16},{2,18},{4,20},{6,22},{8,24},{10,26},{12,28},{14,30},{16,0},... | collective-permute-start | bytes 245768 | tf_op jit(solution)/shard_map/ppermute | solution.py:421
  273.3 16.1 %collective-permute-start.16 = (bf16[160,512]{1,0:T(8,128)(2,1)S(1)}, bf16[160,512]{1,0:T(8,128)(2,1)S(1)}, u32[]{:S(2)}, u32[]{:S(2)}) collective-permute-start(bf16[160,512]{1,0:T(8,128)(2,1)S(1)} %pad_maximum_fusion.19), channel_id=1, source_target_pairs={{0,8},{2,10},{4,12},{6,14},{8,0},{10,2},{12,4},{14,6},{16,24},{18,... | collective-permute-start | bytes 491528 | tf_op jit(solution)/shard_map/ppermute | solution.py:421
  274.6 28.8 %collective-permute-start.38 = (bf16[320,512]{1,0:T(8,128)(2,1)S(1)}, bf16[320,512]{1,0:T(8,128)(2,1)S(1)}, u32[]{:S(2)}, u32[]{:S(2)}) collective-permute-start(bf16[320,512]{1,0:T(8,128)(2,1)S(1)} %pad_maximum_fusion.18), channel_id=1, source_target_pairs={{0,8},{2,10},{4,12},{6,14},{8,0},{10,2},{12,4},{14,6},{16,24},{18,... | collective-permute-start | bytes 983048 | tf_op jit(solution)/shard_map/ppermute | solution.py:421
  275.6 39.3 %collective-permute-start.24 = (bf16[320,512]{1,0:T(8,128)(2,1)S(1)}, bf16[320,512]{1,0:T(8,128)(2,1)S(1)}, u32[]{:S(2)}, u32[]{:S(2)}) collective-permute-start(bf16[320,512]{1,0:T(8,128)(2,1)S(1)} %pad_maximum_fusion.16), channel_id=1, source_target_pairs={{0,8},{2,10},{4,12},{6,14},{8,0},{10,2},{12,4},{14,6},{16,24},{18,... | collective-permute-start | bytes 983048 | tf_op jit(solution)/shard_map/ppermute | solution.py:421
  282.5 32.6 %collective-permute-start.31 = (bf16[320,512]{1,0:T(8,128)(2,1)S(1)}, bf16[320,512]{1,0:T(8,128)(2,1)S(1)}, u32[]{:S(2)}, u32[]{:S(2)}) collective-permute-start(bf16[320,512]{1,0:T(8,128)(2,1)S(1)} %pad_maximum_fusion.17), channel_id=1, source_target_pairs={{0,4},{2,6},{4,0},{6,2},{8,12},{10,14},{12,8},{14,10},{16,20},{18,... | collective-permute-start | bytes 983048 | tf_op jit(solution)/shard_map/ppermute | solution.py:421
  289.5 25.7 %collective-permute-start.17 = (bf16[320,512]{1,0:T(8,128)(2,1)S(1)}, bf16[320,512]{1,0:T(8,128)(2,1)S(1)}, u32[]{:S(2)}, u32[]{:S(2)}) collective-permute-start(bf16[320,512]{1,0:T(8,128)(2,1)S(1)} %pad_maximum_fusion.15), channel_id=1, source_target_pairs={{0,4},{2,6},{4,0},{6,2},{8,12},{10,14},{12,8},{14,10},{16,20},{18,... | collective-permute-start | bytes 983048 | tf_op jit(solution)/shard_map/ppermute | solution.py:421
  347.6 15.1 %collective-permute-start.39 = (bf16[640,512]{1,0:T(8,128)(2,1)S(1)}, bf16[640,512]{1,0:T(8,128)(2,1)S(1)}, u32[]{:S(2)}, u32[]{:S(2)}) collective-permute-start(bf16[640,512]{1,0:T(8,128)(2,1)S(1)} %pad_maximum_fusion.11), channel_id=1, source_target_pairs={{0,2},{2,0},{4,6},{6,4},{8,10},{10,8},{12,14},{14,12},{16,18},{18,... | collective-permute-start | bytes 1966088 | tf_op jit(solution)/shard_map/ppermute | solution.py:421
  347.7 15.3 %collective-permute-start.40 = (bf16[640,512]{1,0:T(8,128)(2,1)S(1)}, bf16[640,512]{1,0:T(8,128)(2,1)S(1)}, u32[]{:S(2)}, u32[]{:S(2)}) collective-permute-start(bf16[640,512]{1,0:T(8,128)(2,1)S(1)} %pad_maximum_fusion.12), channel_id=1, source_target_pairs={{0,2},{2,0},{4,6},{6,4},{8,10},{10,8},{12,14},{14,12},{16,18},{18,... | collective-permute-start | bytes 1966088 | tf_op jit(solution)/shard_map/ppermute | solution.py:421
  350.8 12.7 %collective-permute-start.41 = (bf16[640,512]{1,0:T(8,128)(2,1)S(1)}, bf16[640,512]{1,0:T(8,128)(2,1)S(1)}, u32[]{:S(2)}, u32[]{:S(2)}) collective-permute-start(bf16[640,512]{1,0:T(8,128)(2,1)S(1)} %pad_maximum_fusion.13), channel_id=1, source_target_pairs={{0,2},{2,0},{4,6},{6,4},{8,10},{10,8},{12,14},{14,12},{16,18},{18,... | collective-permute-start | bytes 1966088 | tf_op jit(solution)/shard_map/ppermute | solution.py:421
  350.9 12.9 %collective-permute-start.42 = (bf16[640,512]{1,0:T(8,128)(2,1)S(1)}, bf16[640,512]{1,0:T(8,128)(2,1)S(1)}, u32[]{:S(2)}, u32[]{:S(2)}) collective-permute-start(bf16[640,512]{1,0:T(8,128)(2,1)S(1)} %pad_maximum_fusion.14), channel_id=1, source_target_pairs={{0,2},{2,0},{4,6},{6,4},{8,10},{10,8},{12,14},{14,12},{16,18},{18,... | collective-permute-start | bytes 1966088 | tf_op jit(solution)/shard_map/ppermute | solution.py:421
  (35 other events, 307.1 us)
Sparse Core Ops, SparseCore 0:
  137.5 210.0 all-reduce.4
where the time goes:
time: 388 us; the launch traced here: 380 us
  waiting for transfers between devices  148 us (38%)
  Pallas kernels  73.3 us (19%)
  other arithmetic  42.8 us (11%)
  starting transfers between devices  41.4 us (11%)
  matrix products  39.7 us (10%)
  local copies, waits for them, and re-layouts  18.6 us (5%)
  between operations  16.1 us (4%)
    ppermute x32, waiting for transfers between devices, swap(): return lax.ppermute(array, 'dp', [(i, i ^ bit) for i in range(size)])  87.5 us
    pallas_call x1, Pallas kernels, attend_forward(): pl.pallas_call(functools.partial(fwd_kernel, slots, sp, rp), out_shape=[j...  40.4 us
    pallas_call x1, Pallas kernels, attend_backward(): pl.pallas_call(functools.partial(bwd_kernel, slots, sp, rp, width), grid=...  32.9 us
    psum x1, waiting for transfers between devices, on_device(): ffn_sums = lax.psum((down_grad, up_grad), 'dp')  32.2 us
    ppermute x32, starting transfers between devices, swap(): return lax.ppermute(array, 'dp', [(i, i ^ bit) for i in range(size)])  29.1 us
    ppermute x4, waiting for transfers between devices, total(): lax.ppermute(partial, 'tensor', pair).astype(F32)  19.3 us
    dot_general x6, matrix products, dot_tn(): lax.dot_general(a, b, (((0,), (0,)), ((), ())), preferred_element_type=F32)  15.8 us
    dot_general x6, matrix products, dot_nt(): lax.dot_general(a, b, (((1,), (1,)), ((), ())), preferred_element_type=F32)  12.8 us
  transfers between devices with their start and end apart: 44, of which 23 were waited for; matrix products, arithmetic and copies ran while one was open for 22% of the time, Pallas kernels for 19%

commit v1 on v0

--- a/solution.py
+++ b/solution.py
@@ -344,7 +344,8 @@
             each(rp // tall, gather_back, True)
             acc[side] = jnp.where(mine_down, nn(own_t[:, 0:rp], dns[...]), acc[side])
         return carry
-    lax.fori_loop(0, 2, head, 0)
+    for h in range(2):
+        head(h, 0)
 
     for side in range(2):
         dqkv_ref[:, pl.ds(pl.multiple_of(side * width + pair * 128, 128), 128)] = gs[side, 0:slots, :]

time: 388 us -> 387 us (level)
  transfers between devices with their start and end apart: 44 -> 44, of which waited for: 23 -> 24; matrix products, arithmetic and copies ran while one was open for 22% -> 22% of each run, Pallas kernels for 19% -> 19%
where the time goes in v1:
time: 387 us; the launch traced here: 379 us
  waiting for transfers between devices  149 us (39%)
  Pallas kernels  71.2 us (18%)
  other arithmetic  42.9 us (11%)
  starting transfers between devices  42.1 us (11%)
  matrix products  39.6 us (10%)
  local copies, waits for them, and re-layouts  18.6 us (5%)
  between operations  16.3 us (4%)
    ppermute x32, waiting for transfers between devices, swap(): return lax.ppermute(array, 'dp', [(i, i ^ bit) for i in range(size)])  86.7 us
    pallas_call x1, Pallas kernels, attend_forward(): pl.pallas_call(functools.partial(fwd_kernel, slots, sp, rp), out_shape=[j...  40.4 us
    psum x1, waiting for transfers between devices, on_device(): ffn_sums = lax.psum((down_grad, up_grad), 'dp')  33.4 us
    pallas_call x1, Pallas kernels, attend_backward(): pl.pallas_call(functools.partial(bwd_kernel, slots, sp, rp, width), grid=...  30.8 us
    ppermute x32, starting transfers between devices, swap(): return lax.ppermute(array, 'dp', [(i, i ^ bit) for i in range(size)])  29.8 us
    ppermute x4, waiting for transfers between devices, total(): lax.ppermute(partial, 'tensor', pair).astype(F32)  19.1 us
    dot_general x6, matrix products, dot_tn(): lax.dot_general(a, b, (((0,), (0,)), ((), ())), preferred_element_type=F32)  15.5 us
    dot_general x6, matrix products, dot_nt(): lax.dot_general(a, b, (((1,), (1,)), ((), ())), preferred_element_type=F32)  12.9 us
  transfers between devices with their start and end apart: 44, of which 24 were waited for; matrix products, arithmetic and copies ran while one was open for 22% of the time, Pallas kernels for 19%

profile of v1, /device:TPU:0, one launch (start us, length us, event | category | flops | bytes accessed | tf_op | source)
XLA Modules:
  0.0 379.4 jit_solution(11619404011182008904)
XLA Ops:
  7.2 3.1 collective-permute-start
  19.5 3.2 copy.26
  29.1 3.2 fusion.q_ref.k_ref.v_ref
  32.3 40.4 %attend_forward.1 = (bf16[1,561,512]{2,1,0:T(8,128)(2,1)}, bf16[1,8,576,640]{3,2,1,0:T(8,128)(2,1)}) custom-call(s32[1]{0:T(128)S(6)} %copy.48.len_ref, bf16[1,561,1536]{2,1,0:T(8,128)(2,1)} %fusion.q_ref.k_ref.v_ref, bf16[1,561,1536]{2,1,0:T(8,128)(2,1)} %fusion.q_ref.k_ref.v_ref, bf16[1,561,1536]{2,1,0:T(8,128)(2,1)} %fusion.q_ref.k_ref.v_ref, ...), custom_call_target="tpu_custom_call" | custom-call | tf_op jit(solution)/shard_map/attend_forward/pallas_call | solution.py:207
  77.7 7.4 %collective-permute-done.6 = bf16[273,512]{1,0:T(8,128)(2,1)S(1)} collective-permute-done((bf16[273,512]{1,0:T(8,128)(2,1)S(1)}, bf16[273,512]{1,0:T(8,128)(2,1)S(1)}, u32[]{:S(2)}, u32[]{:S(2)}) %collective-permute-start.6) | collective-permute-done | bytes 279584 | tf_op jit(solution)/shard_map/ppermute | solution.py:486
  97.7 9.3 %collective-permute-done.7 = bf16[273,1024]{1,0:T(8,128)(2,1)S(1)} collective-permute-done((bf16[273,1024]{1,0:T(8,128)(2,1)S(1)}, bf16[273,1024]{1,0:T(8,128)(2,1)S(1)}, u32[]{:S(2)}, u32[]{:S(2)}) %collective-permute-start.7) | collective-permute-done | bytes 559136 | tf_op jit(solution)/shard_map/ppermute | solution.py:494
  109.8 2.5 fusion.2
  114.8 4.6 %collective-permute-done.5 = bf16[288,1024]{1,0:T(8,128)(2,1)S(1)} collective-permute-done((bf16[288,1024]{1,0:T(8,128)(2,1)S(1)}, bf16[288,1024]{1,0:T(8,128)(2,1)S(1)}, u32[]{:S(2)}, u32[]{:S(2)}) %collective-permute-start.5) | collective-permute-done | bytes 589856 | tf_op jit(solution)/shard_map/ppermute | solution.py:494
  122.0 2.3 fusion.1
  126.5 5.0 %convolution_convert_fusion = bf16[1024,2048]{1,0:T(8,128)(2,1)} fusion(bf16[273,2048]{1,0:T(8,128)(2,1)S(1)} %fusion.2, bf16[288,2048]{1,0:T(8,128)(2,1)S(1)} %fusion.1, bf16[273,1024]{1,0:T(8,128)(2,1)S(1)} %fusion.45, bf16[288,1024]{1,0:T(8,128)(2,1)S(1)} %fusion.44), kind=kOutput, calls=%fused_computation.3 | convolution fusion | flops 2361995264 | bytes 7641088 | tf_op jit(solution)/shard_map/dot_general | solution.py:401
  131.5 5.2 %convolution_convert_fusion.1 = bf16[2048,1024]{1,0:T(8,128)(2,1)} fusion(bf16[273,2048]{1,0:T(8,128)(2,1)S(1)} %get-tuple-element.171, bf16[288,2048]{1,0:T(8,128)(2,1)S(1)} %get-tuple-element.168, bf16[273,1024]{1,0:T(8,128)(2,1)S(1)} %get-tuple-element.40, bf16[288,1024]{1,0:T(8,128)(2,1)S(1)} %get-tuple-element.43), kind=kOutput, calls=%fused_computation.4 | convolution fusion | flops 2361995264 | bytes 7641088 | tf_op jit(solution)/shard_map/dot_general | solution.py:401
  141.7 5.3 %collective-permute-done.9 = bf16[288,1024]{1,0:T(8,128)(2,1)} collective-permute-done((bf16[288,1024]{1,0:T(8,128)(2,1)}, bf16[288,1024]{1,0:T(8,128)(2,1)}, u32[]{:S(2)}, u32[]{:S(2)}) %collective-permute-start.9) | collective-permute-done | bytes 589856 | tf_op jit(solution)/shard_map/ppermute | solution.py:494
  153.2 30.8 %attend_backward.1 = (bf16[1,561,1536]{2,1,0:T(8,128)(2,1)}, f32[1,384,512]{2,1,0:T(8,128)}, f32[1,384,512]{2,1,0:T(8,128)}) custom-call(bf16[1,561,1536]{2,1,0:T(8,128)(2,1)} %fusion.q_ref.k_ref.v_ref, bf16[1,561,1536]{2,1,0:T(8,128)(2,1)} %fusion.q_ref.k_ref.v_ref, bf16[1,561,1536]{2,1,0:T(8,128)(2,1)} %fusion.q_ref.k_ref.v_ref, ...), custom_call_target="tpu_custom_call" | custom-call | tf_op jit(solution)/shard_map/attend_backward/pallas_call | solution.py:368
  200.5 5.7 %collective-permute-done.33 = bf16[320,512]{1,0:T(8,128)(2,1)S(1)} collective-permute-done((bf16[320,512]{1,0:T(8,128)(2,1)S(1)}, bf16[320,512]{1,0:T(8,128)(2,1)S(1)}, u32[]{:S(2)}, u32[]{:S(2)}) %collective-permute-start.33) | collective-permute-done | bytes 327712 | tf_op jit(solution)/shard_map/ppermute | solution.py:422
  208.0 9.9 %collective-permute-done.19 = bf16[320,512]{1,0:T(8,128)(2,1)S(1)} collective-permute-done((bf16[320,512]{1,0:T(8,128)(2,1)S(1)}, bf16[320,512]{1,0:T(8,128)(2,1)S(1)}, u32[]{:S(2)}, u32[]{:S(2)}) %collective-permute-start.19) | collective-permute-done | bytes 327712 | tf_op jit(solution)/shard_map/ppermute | solution.py:422
  226.9 2.9 collective-permute-start.35
  232.1 2.8 collective-permute-start.28
  234.9 4.2 %collective-permute-done.13 = bf16[160,512]{1,0:T(8,128)(2,1)S(1)} collective-permute-done((bf16[160,512]{1,0:T(8,128)(2,1)S(1)}, bf16[160,512]{1,0:T(8,128)(2,1)S(1)}, u32[]{:S(2)}, u32[]{:S(2)}) %collective-permute-start.13) | collective-permute-done | bytes 163872 | tf_op jit(solution)/shard_map/ppermute | solution.py:422
  239.3 3.0 collective-permute-start.36
  242.3 4.0 %collective-permute-done.21 = bf16[80,512]{1,0:T(8,128)(2,1)S(1)} collective-permute-done((bf16[80,512]{1,0:T(8,128)(2,1)S(1)}, bf16[80,512]{1,0:T(8,128)(2,1)S(1)}, u32[]{:S(2)}, u32[]{:S(2)}) %collective-permute-start.21) | collective-permute-done | bytes 81952 | tf_op jit(solution)/shard_map/ppermute | solution.py:422
  246.5 8.5 %collective-permute-done.28 = bf16[80,512]{1,0:T(8,128)(2,1)S(1)} collective-permute-done((bf16[80,512]{1,0:T(8,128)(2,1)S(1)}, bf16[80,512]{1,0:T(8,128)(2,1)S(1)}, u32[]{:S(2)}, u32[]{:S(2)}) %collective-permute-start.28) | collective-permute-done | bytes 81952 | tf_op jit(solution)/shard_map/ppermute | solution.py:422
  255.1 5.8 %collective-permute-done.14 = bf16[80,512]{1,0:T(8,128)(2,1)S(1)} collective-permute-done((bf16[80,512]{1,0:T(8,128)(2,1)S(1)}, bf16[80,512]{1,0:T(8,128)(2,1)S(1)}, u32[]{:S(2)}, u32[]{:S(2)}) %collective-permute-start.14) | collective-permute-done | bytes 81952 | tf_op jit(solution)/shard_map/ppermute | solution.py:422
  261.1 6.0 %collective-permute-done.36 = bf16[80,512]{1,0:T(8,128)(2,1)S(1)} collective-permute-done((bf16[80,512]{1,0:T(8,128)(2,1)S(1)}, bf16[80,512]{1,0:T(8,128)(2,1)S(1)}, u32[]{:S(2)}, u32[]{:S(2)}) %collective-permute-start.36) | collective-permute-done | bytes 81952 | tf_op jit(solution)/shard_map/ppermute | solution.py:422
  276.3 3.5 collective-permute-done.30
  280.9 5.9 %collective-permute-done.16 = bf16[160,512]{1,0:T(8,128)(2,1)S(1)} collective-permute-done((bf16[160,512]{1,0:T(8,128)(2,1)S(1)}, bf16[160,512]{1,0:T(8,128)(2,1)S(1)}, u32[]{:S(2)}, u32[]{:S(2)}) %collective-permute-start.16) | collective-permute-done | bytes 163872 | tf_op jit(solution)/shard_map/ppermute | solution.py:422
  287.9 12.9 %collective-permute-done.38 = bf16[320,512]{1,0:T(8,128)(2,1)S(1)} collective-permute-done((bf16[320,512]{1,0:T(8,128)(2,1)S(1)}, bf16[320,512]{1,0:T(8,128)(2,1)S(1)}, u32[]{:S(2)}, u32[]{:S(2)}) %collective-permute-start.38) | collective-permute-done | bytes 327712 | tf_op jit(solution)/shard_map/ppermute | solution.py:422
  301.0 11.5 %collective-permute-done.24 = bf16[320,512]{1,0:T(8,128)(2,1)S(1)} collective-permute-done((bf16[320,512]{1,0:T(8,128)(2,1)S(1)}, bf16[320,512]{1,0:T(8,128)(2,1)S(1)}, u32[]{:S(2)}, u32[]{:S(2)}) %collective-permute-start.24) | collective-permute-done | bytes 327712 | tf_op jit(solution)/shard_map/ppermute | solution.py:422
  313.0 33.4 %all-reduce.5.cloned.1.call-done = (bf16[2048,1024]{1,0:T(8,128)(2,1)}, bf16[1024,2048]{1,0:T(8,128)(2,1)}) async-done(((bf16[2048,1024]{1,0:T(8,128)(2,1)}, bf16[1024,2048]{1,0:T(8,128)(2,1)}), (bf16[2048,1024]{1,0:T(8,128)(2,1)}, bf16[1024,2048]{1,0:T(8,128)(2,1)})) %all-reduce.5.cloned.1.call-update) | async-done | bytes 8388624 | tf_op jit(solution)/shard_map/psum | solution.py:565
  346.9 2.6 fusion.55
  350.1 6.8 %convert_element_type.394 = f32[1024,2048]{1,0:T(8,128)} convert(bf16[1024,2048]{1,0:T(8,128)(2,1)} %get-tuple-element.54) | non-fusion elementwise | flops 2097152 | bytes 12582912 | tf_op jit(solution)/shard_map/convert_element_type | solution.py:603
  356.9 4.7 %convert_element_type.395 = f32[2048,1024]{1,0:T(8,128)} convert(bf16[2048,1024]{1,0:T(8,128)(2,1)S(1)} %copy-done.3) | non-fusion elementwise | flops 2097152 | bytes 12582912 | tf_op jit(solution)/shard_map/convert_element_type | solution.py:604
  368.7 3.4 pad_maximum_fusion
  (250 shorter events, 103.3 us)
Async XLA Ops:
  7.2 339.2 %all-reduce.5.cloned.1.call-start = ((), (), s32[]{:S(2)}) async-start(), calls=%async_computation | async-start | bytes 16777216 | tf_op jit(solution)/shard_map/psum | solution.py:565
  7.2 17.5 %collective-permute-start = (bf16[561,512]{1,0:T(8,128)(2,1)}, bf16[561,512]{1,0:T(8,128)(2,1)}, u32[]{:S(2)}, u32[]{:S(2)}) collective-permute-start(bf16[561,512]{1,0:T(8,128)(2,1)} %bitcast.97), channel_id=1, source_target_pairs={{0,1},{1,0},{2,3},{3,2},{4,5},{5,4},{6,7},{7,6},{8,9},{9,8},{10,11... | collective-permute-start | bytes 1723400 | tf_op jit(solution)/shard_map/ppermute | solution.py:486
  11.0 13.7 %collective-permute-start.2 = (f32[4,512]{1,0:T(4,128)S(1)}, f32[4,512]{1,0:T(4,128)S(1)}, u32[]{:S(2)}, u32[]{:S(2)}) collective-permute-start(f32[4,512]{1,0:T(4,128)S(1)} %pad_maximum_fusion.24), channel_id=1, source_target_pairs={{0,1},{1,0},{2,3},{3,2},{4,5},{5,4},{6,7},{7,6},{8,9},{9,8},{10,11... | collective-permute-start | bytes 24584 | tf_op jit(solution)/shard_map/ppermute | solution.py:486
  11.1 61.7 %collective-permute-start.3 = (bf16[512,1024]{1,0:T(8,128)(2,1)}, bf16[512,1024]{1,0:T(8,128)(2,1)}, u32[]{:S(2)}, u32[]{:S(2)}) collective-permute-start(bf16[512,1024]{1,0:T(8,128)(2,1)} %param.16), channel_id=1, source_target_pairs={{0,1},{1,0},{2,3},{3,2},{4,5},{5,4},{6,7},{7,6},{8,9},{9,8},{10,11... | collective-permute-start | bytes 3145736 | tf_op jit(solution)/shard_map/ppermute | solution.py:486
  27.1 47.2 %collective-permute-start.1 = (bf16[561,512]{1,0:T(8,128)(2,1)S(1)}, bf16[561,512]{1,0:T(8,128)(2,1)S(1)}, u32[]{:S(2)}, u32[]{:S(2)}) collective-permute-start(bf16[561,512]{1,0:T(8,128)(2,1)S(1)} %bitcast.98), channel_id=1, source_target_pairs={{0,1},{1,0},{2,3},{3,2},{4,5},{5,4},{6,7},{7,6},{8,9},{9,8},{10,11... | collective-permute-start | bytes 1723400 | tf_op jit(solution)/shard_map/ppermute | solution.py:486
  75.6 15.6 %collective-permute-start.4 = (bf16[288,512]{1,0:T(8,128)(2,1)S(1)}, bf16[288,512]{1,0:T(8,128)(2,1)S(1)}, u32[]{:S(2)}, u32[]{:S(2)}) collective-permute-start(bf16[288,512]{1,0:T(8,128)(2,1)S(1)} %slice_bitcast_fusion.3), channel_id=1, source_target_pairs={{0,1},{1,0},{2,3},{3,2},{4,5},{5,4},{6,7},{7,6},{8,9},{9,8},{10,11... | collective-permute-start | bytes 884744 | tf_op jit(solution)/shard_map/ppermute | solution.py:486
  91.0 15.9 %collective-permute-start.7 = (bf16[273,1024]{1,0:T(8,128)(2,1)S(1)}, bf16[273,1024]{1,0:T(8,128)(2,1)S(1)}, u32[]{:S(2)}, u32[]{:S(2)}) collective-permute-start(bf16[273,1024]{1,0:T(8,128)(2,1)S(1)} %convolution_convert_fusion.12), channel_id=1, source_target_pairs={{0,1},{1,0},{2,3},{3,2},{4,5},{5,4},{6,7},{7,6},{8,9},{9,8},{10,11... | collective-permute-start | bytes 1677320 | tf_op jit(solution)/shard_map/ppermute | solution.py:494
  95.7 23.7 %collective-permute-start.5 = (bf16[288,1024]{1,0:T(8,128)(2,1)S(1)}, bf16[288,1024]{1,0:T(8,128)(2,1)S(1)}, u32[]{:S(2)}, u32[]{:S(2)}) collective-permute-start(bf16[288,1024]{1,0:T(8,128)(2,1)S(1)} %convolution_convert_fusion.9), channel_id=1, source_target_pairs={{0,1},{1,0},{2,3},{3,2},{4,5},{5,4},{6,7},{7,6},{8,9},{9,8},{10,11... | collective-permute-start | bytes 1769480 | tf_op jit(solution)/shard_map/ppermute | solution.py:494
  114.6 24.4 %collective-permute-start.8 = (bf16[273,1024]{1,0:T(8,128)(2,1)}, bf16[273,1024]{1,0:T(8,128)(2,1)}, u32[]{:S(2)}, u32[]{:S(2)}) collective-permute-start(bf16[273,1024]{1,0:T(8,128)(2,1)} %convolution_convert_fusion.11), channel_id=1, source_target_pairs={{0,1},{1,0},{2,3},{3,2},{4,5},{5,4},{6,7},{7,6},{8,9},{9,8},{10,11... | collective-permute-start | bytes 1677320 | tf_op jit(solution)/shard_map/ppermute | solution.py:494
  194.1 152.8 %collective-permute-start.10 = (bf16[561,512]{1,0:T(8,128)(2,1)S(1)}, bf16[561,512]{1,0:T(8,128)(2,1)}, u32[]{:S(2)}, u32[]{:S(2)}) collective-permute-start(bf16[561,512]{1,0:T(8,128)(2,1)S(1)} %constant_dynamic-slice_fusion), channel_id=1, source_target_pairs={{0,1},{1,0},{2,3},{3,2},{4,5},{5,4},{6,7},{7,6},{8,9},{9,8},{10,11... | collective-permute-start | bytes 1723400 | tf_op jit(solution)/shard_map/ppermute | solution.py:503
  197.4 20.5 %collective-permute-start.19 = (bf16[320,512]{1,0:T(8,128)(2,1)S(1)}, bf16[320,512]{1,0:T(8,128)(2,1)S(1)}, u32[]{:S(2)}, u32[]{:S(2)}) collective-permute-start(bf16[320,512]{1,0:T(8,128)(2,1)S(1)} %broadcast_select_fusion.15), channel_id=1, source_target_pairs={{0,8},{2,10},{4,12},{6,14},{8,0},{10,2},{12,4},{14,6},{16,24},{18,... | collective-permute-start | bytes 983048 | tf_op jit(solution)/shard_map/ppermute | solution.py:422
  198.0 21.8 %collective-permute-start.26 = (bf16[320,512]{1,0:T(8,128)(2,1)S(1)}, bf16[320,512]{1,0:T(8,128)(2,1)S(1)}, u32[]{:S(2)}, u32[]{:S(2)}) collective-permute-start(bf16[320,512]{1,0:T(8,128)(2,1)S(1)} %broadcast_select_fusion.18), channel_id=1, source_target_pairs={{0,4},{2,6},{4,0},{6,2},{8,12},{10,14},{12,8},{14,10},{16,20},{18,... | collective-permute-start | bytes 983048 | tf_op jit(solution)/shard_map/ppermute | solution.py:422
  200.1 23.1 %collective-permute-start.12 = (bf16[320,512]{1,0:T(8,128)(2,1)S(1)}, bf16[320,512]{1,0:T(8,128)(2,1)S(1)}, u32[]{:S(2)}, u32[]{:S(2)}) collective-permute-start(bf16[320,512]{1,0:T(8,128)(2,1)S(1)} %broadcast_select_fusion.21), channel_id=1, source_target_pairs={{0,4},{2,6},{4,0},{6,2},{8,12},{10,14},{12,8},{14,10},{16,20},{18,... | collective-permute-start | bytes 983048 | tf_op jit(solution)/shard_map/ppermute | solution.py:422
  206.4 20.4 %collective-permute-start.34 = (bf16[160,512]{1,0:T(8,128)(2,1)S(1)}, bf16[160,512]{1,0:T(8,128)(2,1)S(1)}, u32[]{:S(2)}, u32[]{:S(2)}) collective-permute-start(bf16[160,512]{1,0:T(8,128)(2,1)S(1)} %broadcast_select_fusion.28), channel_id=1, source_target_pairs={{0,4},{2,6},{4,0},{6,2},{8,12},{10,14},{12,8},{14,10},{16,20},{18,... | collective-permute-start | bytes 491528 | tf_op jit(solution)/shard_map/ppermute | solution.py:422
  220.0 12.0 %collective-permute-start.27 = (bf16[160,512]{1,0:T(8,128)(2,1)S(1)}, bf16[160,512]{1,0:T(8,128)(2,1)S(1)}, u32[]{:S(2)}, u32[]{:S(2)}) collective-permute-start(bf16[160,512]{1,0:T(8,128)(2,1)S(1)} %broadcast_select_fusion.34), channel_id=1, source_target_pairs={{0,8},{2,10},{4,12},{6,14},{8,0},{10,2},{12,4},{14,6},{16,24},{18,... | collective-permute-start | bytes 491528 | tf_op jit(solution)/shard_map/ppermute | solution.py:422
  223.4 15.8 %collective-permute-start.13 = (bf16[160,512]{1,0:T(8,128)(2,1)S(1)}, bf16[160,512]{1,0:T(8,128)(2,1)S(1)}, u32[]{:S(2)}, u32[]{:S(2)}) collective-permute-start(bf16[160,512]{1,0:T(8,128)(2,1)S(1)} %broadcast_select_fusion.37), channel_id=1, source_target_pairs={{0,8},{2,10},{4,12},{6,14},{8,0},{10,2},{12,4},{14,6},{16,24},{18,... | collective-permute-start | bytes 491528 | tf_op jit(solution)/shard_map/ppermute | solution.py:422
  226.9 12.4 %collective-permute-start.35 = (bf16[80,512]{1,0:T(8,128)(2,1)S(1)}, bf16[80,512]{1,0:T(8,128)(2,1)S(1)}, u32[]{:S(2)}, u32[]{:S(2)}) collective-permute-start(bf16[80,512]{1,0:T(8,128)(2,1)S(1)} %broadcast_select_fusion.40), channel_id=1, source_target_pairs={{0,16},{2,18},{4,20},{6,22},{8,24},{10,26},{12,28},{14,30},{16,0},... | collective-permute-start | bytes 245768 | tf_op jit(solution)/shard_map/ppermute | solution.py:422
  229.8 16.5 %collective-permute-start.21 = (bf16[80,512]{1,0:T(8,128)(2,1)S(1)}, bf16[80,512]{1,0:T(8,128)(2,1)S(1)}, u32[]{:S(2)}, u32[]{:S(2)}) collective-permute-start(bf16[80,512]{1,0:T(8,128)(2,1)S(1)} %broadcast_select_fusion.46), channel_id=1, source_target_pairs={{0,16},{2,18},{4,20},{6,22},{8,24},{10,26},{12,28},{14,30},{16,0},... | collective-permute-start | bytes 245768 | tf_op jit(solution)/shard_map/ppermute | solution.py:422
  232.1 22.9 %collective-permute-start.28 = (bf16[80,512]{1,0:T(8,128)(2,1)S(1)}, bf16[80,512]{1,0:T(8,128)(2,1)S(1)}, u32[]{:S(2)}, u32[]{:S(2)}) collective-permute-start(bf16[80,512]{1,0:T(8,128)(2,1)S(1)} %broadcast_select_fusion.43), channel_id=1, source_target_pairs={{0,16},{2,18},{4,20},{6,22},{8,24},{10,26},{12,28},{14,30},{16,0},... | collective-permute-start | bytes 245768 | tf_op jit(solution)/shard_map/ppermute | solution.py:422
  239.2 21.7 %collective-permute-start.14 = (bf16[80,512]{1,0:T(8,128)(2,1)S(1)}, bf16[80,512]{1,0:T(8,128)(2,1)S(1)}, u32[]{:S(2)}, u32[]{:S(2)}) collective-permute-start(bf16[80,512]{1,0:T(8,128)(2,1)S(1)} %broadcast_select_fusion.49), channel_id=1, source_target_pairs={{0,16},{2,18},{4,20},{6,22},{8,24},{10,26},{12,28},{14,30},{16,0},... | collective-permute-start | bytes 245768 | tf_op jit(solution)/shard_map/ppermute | solution.py:422
  239.3 27.7 %collective-permute-start.36 = (bf16[80,512]{1,0:T(8,128)(2,1)S(1)}, bf16[80,512]{1,0:T(8,128)(2,1)S(1)}, u32[]{:S(2)}, u32[]{:S(2)}) collective-permute-start(bf16[80,512]{1,0:T(8,128)(2,1)S(1)} %add_convert_fusion.14), channel_id=1, source_target_pairs={{0,16},{2,18},{4,20},{6,22},{8,24},{10,26},{12,28},{14,30},{16,0},... | collective-permute-start | bytes 245768 | tf_op jit(solution)/shard_map/ppermute | solution.py:422
  246.4 22.7 %collective-permute-start.22 = (bf16[80,512]{1,0:T(8,128)(2,1)S(1)}, bf16[80,512]{1,0:T(8,128)(2,1)S(1)}, u32[]{:S(2)}, u32[]{:S(2)}) collective-permute-start(bf16[80,512]{1,0:T(8,128)(2,1)S(1)} %add_convert_fusion.16), channel_id=1, source_target_pairs={{0,16},{2,18},{4,20},{6,22},{8,24},{10,26},{12,28},{14,30},{16,0},... | collective-permute-start | bytes 245768 | tf_op jit(solution)/shard_map/ppermute | solution.py:422
  255.0 15.8 %collective-permute-start.29 = (bf16[80,512]{1,0:T(8,128)(2,1)S(1)}, bf16[80,512]{1,0:T(8,128)(2,1)S(1)}, u32[]{:S(2)}, u32[]{:S(2)}) collective-permute-start(bf16[80,512]{1,0:T(8,128)(2,1)S(1)} %add_convert_fusion.15), channel_id=1, source_target_pairs={{0,16},{2,18},{4,20},{6,22},{8,24},{10,26},{12,28},{14,30},{16,0},... | collective-permute-start | bytes 245768 | tf_op jit(solution)/shard_map/ppermute | solution.py:422
  271.9 14.9 %collective-permute-start.16 = (bf16[160,512]{1,0:T(8,128)(2,1)S(1)}, bf16[160,512]{1,0:T(8,128)(2,1)S(1)}, u32[]{:S(2)}, u32[]{:S(2)}) collective-permute-start(bf16[160,512]{1,0:T(8,128)(2,1)S(1)} %pad_maximum_fusion.19), channel_id=1, source_target_pairs={{0,8},{2,10},{4,12},{6,14},{8,0},{10,2},{12,4},{14,6},{16,24},{18,... | collective-permute-start | bytes 491528 | tf_op jit(solution)/shard_map/ppermute | solution.py:422
  274.0 26.8 %collective-permute-start.38 = (bf16[320,512]{1,0:T(8,128)(2,1)S(1)}, bf16[320,512]{1,0:T(8,128)(2,1)S(1)}, u32[]{:S(2)}, u32[]{:S(2)}) collective-permute-start(bf16[320,512]{1,0:T(8,128)(2,1)S(1)} %pad_maximum_fusion.18), channel_id=1, source_target_pairs={{0,8},{2,10},{4,12},{6,14},{8,0},{10,2},{12,4},{14,6},{16,24},{18,... | collective-permute-start | bytes 983048 | tf_op jit(solution)/shard_map/ppermute | solution.py:422
  275.8 36.7 %collective-permute-start.24 = (bf16[320,512]{1,0:T(8,128)(2,1)S(1)}, bf16[320,512]{1,0:T(8,128)(2,1)S(1)}, u32[]{:S(2)}, u32[]{:S(2)}) collective-permute-start(bf16[320,512]{1,0:T(8,128)(2,1)S(1)} %pad_maximum_fusion.16), channel_id=1, source_target_pairs={{0,8},{2,10},{4,12},{6,14},{8,0},{10,2},{12,4},{14,6},{16,24},{18,... | collective-permute-start | bytes 983048 | tf_op jit(solution)/shard_map/ppermute | solution.py:422
  279.8 32.8 %collective-permute-start.31 = (bf16[320,512]{1,0:T(8,128)(2,1)S(1)}, bf16[320,512]{1,0:T(8,128)(2,1)S(1)}, u32[]{:S(2)}, u32[]{:S(2)}) collective-permute-start(bf16[320,512]{1,0:T(8,128)(2,1)S(1)} %pad_maximum_fusion.17), channel_id=1, source_target_pairs={{0,4},{2,6},{4,0},{6,2},{8,12},{10,14},{12,8},{14,10},{16,20},{18,... | collective-permute-start | bytes 983048 | tf_op jit(solution)/shard_map/ppermute | solution.py:422
  286.9 25.9 %collective-permute-start.17 = (bf16[320,512]{1,0:T(8,128)(2,1)S(1)}, bf16[320,512]{1,0:T(8,128)(2,1)S(1)}, u32[]{:S(2)}, u32[]{:S(2)}) collective-permute-start(bf16[320,512]{1,0:T(8,128)(2,1)S(1)} %pad_maximum_fusion.15), channel_id=1, source_target_pairs={{0,4},{2,6},{4,0},{6,2},{8,12},{10,14},{12,8},{14,10},{16,20},{18,... | collective-permute-start | bytes 983048 | tf_op jit(solution)/shard_map/ppermute | solution.py:422
  346.4 15.2 %collective-permute-start.39 = (bf16[640,512]{1,0:T(8,128)(2,1)S(1)}, bf16[640,512]{1,0:T(8,128)(2,1)S(1)}, u32[]{:S(2)}, u32[]{:S(2)}) collective-permute-start(bf16[640,512]{1,0:T(8,128)(2,1)S(1)} %pad_maximum_fusion.11), channel_id=1, source_target_pairs={{0,2},{2,0},{4,6},{6,4},{8,10},{10,8},{12,14},{14,12},{16,18},{18,... | collective-permute-start | bytes 1966088 | tf_op jit(solution)/shard_map/ppermute | solution.py:422
  346.5 15.4 %collective-permute-start.40 = (bf16[640,512]{1,0:T(8,128)(2,1)S(1)}, bf16[640,512]{1,0:T(8,128)(2,1)S(1)}, u32[]{:S(2)}, u32[]{:S(2)}) collective-permute-start(bf16[640,512]{1,0:T(8,128)(2,1)S(1)} %pad_maximum_fusion.12), channel_id=1, source_target_pairs={{0,2},{2,0},{4,6},{6,4},{8,10},{10,8},{12,14},{14,12},{16,18},{18,... | collective-permute-start | bytes 1966088 | tf_op jit(solution)/shard_map/ppermute | solution.py:422
  349.5 12.7 %collective-permute-start.41 = (bf16[640,512]{1,0:T(8,128)(2,1)S(1)}, bf16[640,512]{1,0:T(8,128)(2,1)S(1)}, u32[]{:S(2)}, u32[]{:S(2)}) collective-permute-start(bf16[640,512]{1,0:T(8,128)(2,1)S(1)} %pad_maximum_fusion.13), channel_id=1, source_target_pairs={{0,2},{2,0},{4,6},{6,4},{8,10},{10,8},{12,14},{14,12},{16,18},{18,... | collective-permute-start | bytes 1966088 | tf_op jit(solution)/shard_map/ppermute | solution.py:422
  349.7 13.0 %collective-permute-start.42 = (bf16[640,512]{1,0:T(8,128)(2,1)S(1)}, bf16[640,512]{1,0:T(8,128)(2,1)S(1)}, u32[]{:S(2)}, u32[]{:S(2)}) collective-permute-start(bf16[640,512]{1,0:T(8,128)(2,1)S(1)} %pad_maximum_fusion.14), channel_id=1, source_target_pairs={{0,2},{2,0},{4,6},{6,4},{8,10},{10,8},{12,14},{14,12},{16,18},{18,... | collective-permute-start | bytes 1966088 | tf_op jit(solution)/shard_map/ppermute | solution.py:422
  (35 other events, 301.2 us)
Sparse Core Ops, SparseCore 0:
  137.2 209.1 all-reduce.4
